TPU v7x, 128 devices: a whole 4x4x4 slice. The times are simulated.
128 devices in a mesh: atom: 16 (over y, x), mode: 8 (over z, core).
Axes of the slice: x: 4, y: 4, z: 4, core: 2. Of those that a mesh axis runs over, the one named last changes fastest.
Arguments:
- eigvec: bfloat16 [3, 4096, 2048], P(None, 'atom', 'mode'), may hold values from -0.0546875 to 0.0546875
- force: float32 [3, 3, 16, 4096], P(None, None, None, 'atom'), may hold values from -12 to 12
- bond: float32 [3, 16, 4096], P(None, None, 'atom'), may hold values from -6 to 6
- nbr: int32 [16, 4096], P(None, 'atom'), may hold values from 0 to 4095, as said below
- band: int32 [2, 2048], P(None, 'mode'), may hold values from 0 to 2048, as said below
- freq: float32 [2048], P('mode'), may hold values from 0.5 to 4, as said below
Outputs:
- diffusivity: float32 [2048], P('mode')
- conductivity: float32 [2048], P('mode')
Inputs may be any that keep to these rules, and one draw needn't show every extreme that they name: `nbr`: each entry is an atom whose position in atom order differs from that of its own atom by 1 to 128, counted cyclically over the 4096 atoms; the distance 128 occurs in every draw. For every mode i: max(0, i - 128) <= band[0, i] <= i < band[1, i] <= min(2048, i + 129); both outer limits are reached at some mode. `freq`: strictly increasing along the modes.
All inputs are finite; a program needn't handle non-finite values.
Results may differ from a plain program's by a relative error of at most 0.00057.
Values may be sent and summed in bfloat16 or wider, within the bound.
A program may use at most 64 MiB of HBM per device.

v0:
```python
import math
import jax
import jax.numpy as jnp
from jax import lax
from jax.sharding import PartitionSpec as P

ATOM_DEV = 256
MODE_DEV = 256
RIM = 128
HALF = 128
BROAD = 128


def extended(shard, sides, width, wrap):
    for axis, dim in sides:
        size, length = (lax.axis_size(axis), shard.shape[dim])
        up = [(i, (i + 1) % size) for i in range(size if wrap else size - 1)]
        down = [(j, i) for i, j in up]
        last = lax.slice_in_dim(shard, length - width, length, axis=dim)
        first = lax.slice_in_dim(shard, 0, width, axis=dim)
        before = lax.ppermute(last, axis, up)
        after = lax.ppermute(first, axis, down)
        shard = jnp.concatenate([before, shard, after], axis=dim)
    return shard


def prefix(part, axis, combine, identity):
    place = lax.axis_index(axis)
    gathered = lax.all_gather(part, axis)
    state = jnp.zeros_like(part) + jnp.asarray(identity, part.dtype)

    def one(lap, state):
        return combine(state, lax.dynamic_index_in_dim(gathered, lap, 0, False))

    return lax.fori_loop(0, place, one, state)


def capacity_of(spectral):
    return spectral * spectral * jnp.exp(spectral) / jnp.expm1(spectral) ** 2


def pair_weight(own_freq, partner_freq, own_ids, partner_ids, lower_end, upper_end, broaden):
    inside = (
        (partner_ids[:, None] >= lower_end[None, :])
        & (partner_ids[:, None] < upper_end[None, :])
        & (partner_ids[:, None] != own_ids[None, :])
    )
    detune = own_freq[None, :] - partner_freq[:, None]
    lorentz = broaden / math.pi / (detune * detune + broaden * broaden)
    factor = (own_freq[None, :] + partner_freq[:, None]) ** 2 / (
        4.0 * own_freq[None, :] * partner_freq[:, None]
    )
    return jnp.where(inside, lorentz * factor, 0.0)


def add_totals(earlier, later):
    return earlier + later


def body(eigvec, force, bond, nbr, band, freq):
    atom_count = ATOM_DEV * lax.axis_size("atom")
    mode_count = MODE_DEV * lax.axis_size("mode")
    partner_span = MODE_DEV + 2 * HALF
    spectrum = lax.all_gather(freq, "mode", axis=0, tiled=True)
    atom_rows = extended(eigvec, (("atom", 1),), RIM, True)
    band_rows = extended(eigvec, (("mode", 2),), HALF, False)
    row_major = jnp.transpose(atom_rows, (1, 0, 2))
    domain = lax.axis_index("atom")
    local_ids = (nbr - domain * ATOM_DEV + RIM + atom_count) % atom_count
    block_size = min(512, ATOM_DEV)
    gathered = jnp.take(row_major, local_ids, axis=0)
    coupling = (bond[:, None, None, :, 0:block_size] * force[None, :, :, :, 0:block_size]).astype(
        jnp.bfloat16
    )
    block_image = jnp.einsum(
        "kcdna,nadi->kcai", coupling, gathered, preferred_element_type=jnp.float32
    )
    pieces = block_image.astype(jnp.bfloat16)
    pair_terms = jnp.einsum("caj,kcai->kji", band_rows, pieces, preferred_element_type=jnp.float32)
    mode_block = lax.axis_index("mode")
    mode_start = mode_block * MODE_DEV
    broaden = BROAD * (jnp.max(spectrum) - jnp.min(spectrum)) / (mode_count - 1)
    padded_freq = jnp.pad(spectrum, (HALF, HALF), constant_values=1.0)
    partner_freq = lax.dynamic_slice_in_dim(padded_freq, mode_start, partner_span)
    partner_ids = mode_start - HALF + jnp.arange(partner_span, dtype=jnp.int32)
    own_ids = mode_start + jnp.arange(MODE_DEV, dtype=jnp.int32)
    weight = pair_weight(freq, partner_freq, own_ids, partner_ids, band[0], band[1], broaden)
    summed_pair = lax.psum(pair_terms, "atom")
    strength = jnp.sum(summed_pair * summed_pair, axis=0)
    row_sums = jnp.sum(weight * strength, axis=0)
    diffusivity = math.pi / (3.0 * freq * freq) * row_sums
    running = jnp.cumsum(capacity_of(freq) * diffusivity)
    device_total = running[-1]
    earlier_sum = prefix(device_total, "mode", add_totals, jnp.float32(0.0))
    conductivity = (earlier_sum + running) / MODE_DEV
    return (diffusivity, conductivity)


def solution(mesh):
    in_specs = (
        P(None, "atom", "mode"),
        P(None, None, None, "atom"),
        P(None, None, "atom"),
        P(None, "atom"),
        P(None, "mode"),
        P("mode"),
    )
    out_specs = (P("mode"), P("mode"))
    return jax.shard_map(body, mesh=mesh, in_specs=in_specs, out_specs=out_specs, check_vma=False)
```

profile of v0, /device:TPU:97, one launch (start us, length us, event | category | flops | bytes accessed | tf_op | source)
XLA Modules:
  0.0 190.9 jit_solution(17926169755393144528)
XLA Ops:
  7.2 1.4 copy.12
  8.8 5.0 %collective-permute-start.1 = (bf16[3,128,256]{2,0,1:T(4,128)(2,1)S(1)}, bf16[3,128,256]{2,0,1:T(4,128)(2,1)}, u32[]{:S(2)}, u32[]{:S(2)}) collective-permute-start(bf16[3,128,256]{2,0,1:T(4,128)(2,1)S(1)} %get-tuple-element.39), channel_id=1, source_target_pairs={{8,0},{16,8},{24,16},{32,24},{40,32},{48,40},{56,48},{64,56},{72,6... | collective-permute-start | bytes 589832 | tf_op jit(solution)/shard_map/ppermute | solution.py:22
  13.8 0.8 fusion.22
  14.7 3.5 %collective-permute-start.3 = (bf16[3,256,128]{2,1,0:T(8,128)(2,1)}, bf16[3,256,128]{2,1,0:T(8,128)(2,1)}, u32[]{:S(2)}, u32[]{:S(2)}) collective-permute-start(bf16[3,256,128]{2,1,0:T(8,128)(2,1)} %get-tuple-element.41), channel_id=1, source_target_pairs={{1,0},{2,1},{3,2},{4,3},{5,4},{6,5},{7,6},{9,8},{10,9},{11,10},{12... | collective-permute-start | bytes 589832 | tf_op jit(solution)/shard_map/ppermute | solution.py:22
  18.2 1.3 collective-permute-start.2
  19.6 0.7 copy.17
  20.3 1.1 copy.16
  21.4 0.7 copy.11
  22.1 2.1 %collective-permute-done = bf16[3,128,256]{2,0,1:T(4,128)(2,1)} collective-permute-done((bf16[3,128,256]{2,0,1:T(4,128)(2,1)S(1)}, bf16[3,128,256]{2,0,1:T(4,128)(2,1)}, u32[]{:S(2)}, u32[]{:S(2)}) %collective-permute-start) | collective-permute-done | bytes 196640 | tf_op jit(solution)/shard_map/ppermute | solution.py:21
  24.2 1.8 maximum_bitcast_fusion
  25.9 32.8 %gather_fusion = bf16[4096,3,256]{2,1,0:T(4,128)(2,1)} fusion(bf16[512,3,256]{2,1,0:T(4,128)(2,1)S(1)} %maximum_bitcast_fusion, s32[4096]{0:T(1024)S(1)} %broadcast_clamp_fusion), kind=kCustom, calls=%fused_computation | custom fusion | bytes 12599296 | tf_op jit(solution)/shard_map/jit(_take)/gather | solution.py:71
  58.7 9.2 %fusion.8 = bf16[3,3,256,256]{3,1,0,2:T(4,128)(2,1)S(1)} fusion(f32[3,3,16,256]{2,0,1,3:T(4,128)S(1)} %copy.17, f32[3,16,256]{1,0,2:T(4,128)S(1)} %copy-done.1, bf16[16,256,3,256]{3,2,1,0:T(4,128)(2,1)} %bitcast.42, pred[16,256]{0,1:T(8,128)(4,1)} %copy.11), kind=kOutput, calls=%fused_computation.11 | convolution fusion | flops 60579840 | bytes 7671808 | tf_op jit(solution)/shard_map/kcdna,nadi->kcai/dot_general | solution.py:75
  68.0 3.0 %convolution_bitcast_fusion = f32[3,512,256]{1,2,0:T(8,128)} fusion(bf16[3,3,256,256]{3,1,0,2:T(4,128)(2,1)S(1)} %fusion.8, bf16[3,256,128]{2,1,0:T(8,128)(2,1)} %collective-permute-done.3, bf16[3,256,256]{2,1,0:T(8,128)(2,1)S(1)} %copy-done, bf16[3,256,128]{2,1,0:T(8,128)(2,1)} %collective-permute-done.2), kind=kOutput, calls=%fused_computation.12 | convolution fusion | flops 606339072 | bytes 3538944 | tf_op jit(solution)/shard_map/caj,kcai->kji/dot_general | solution.py:79
  71.0 0.6 copy-done.5
  71.6 8.7 %all-gather = f32[8,1,256]{2,1,0:T(1,128)S(1)} all-gather(f32[1,1,256]{2,1,0:T(1,128)S(1)} %bitcast.45), channel_id=1, replica_groups=mesh['atom'=16,'mode'=8] {'mode'}, dimensions={0}, use_global_device_ids=true | all-gather | bytes 9216 | tf_op jit(solution)/shard_map/all_gather | solution.py:64
  80.3 0.6 fusion.20
  82.3 0.6 dynamic-slice
  83.0 74.9 %all-reduce.4.cloned.1.call-done = f32[3,512,256]{1,2,0:T(8,128)} async-done(((f32[3,512,256]{1,2,0:T(8,128)}), f32[3,512,256]{1,2,0:T(8,128)}) %all-reduce.4.cloned.1.call-update) | async-done | bytes 1572880 | tf_op jit(solution)/shard_map/psum | solution.py:88
  157.8 1.6 multiply_reduce_fusion
  159.5 0.5 multiply_reduce_fusion.1
  160.0 0.6 multiply_bitcast_fusion
  161.2 0.8 slice_dynamic-update-slice_fusion
  162.0 11.9 %all-reduce.1 = f32[8]{0:T(128)S(1)} all-reduce(f32[8]{0:T(128)S(1)} %slice_dynamic-update-slice_fusion), channel_id=1, replica_groups=mesh['atom'=16,'mode'=8] {'mode'}, use_global_device_ids=true, to_apply=%add.1 | all-reduce | flops 8 | bytes 64
  173.8 9.7 %while.10 = (s32[]{:T(128)}, f32[]{:T(128)}, s32[]{:T(128)}, f32[8]{0:T(128)S(1)}, s32[]{:T(128)}, /*index=5*/s32[]{:T(128)}, s32[]{:T(128)}) while((s32[]{:T(128)}, f32[]{:T(128)}, s32[]{:T(128)}, f32[8]{0:T(128)S(1)}, s32[]{:T(128)}, /*index=5*/s32[]{:T(128)}, s32[]{:T(128)}) %tuple.27), condition=%wide.region_8.9_spmd, body=%wide.region_7.8_spmd.sunk | while | flops 6 | bytes 143 | solution.py:35
  173.8 0.7 dynamic_slice.10
  175.2 0.7 dynamic_slice.10
  176.6 0.7 dynamic_slice.10
  178.0 0.7 dynamic_slice.10
  179.4 0.7 dynamic_slice.10
  180.8 0.7 dynamic_slice.10
  182.1 0.7 dynamic_slice.10
  183.5 0.6 add_multiply_fusion
  (37 shorter events, 1.0 us)
Async XLA Ops:
  7.2 6.7 %copy-start = (bf16[3,256,256]{2,1,0:T(8,128)(2,1)S(1)}, bf16[3,256,256]{2,1,0:T(8,128)(2,1)}, u32[]{:S(2)}) copy-start(bf16[3,256,256]{2,1,0:T(8,128)(2,1)} %param.8) | copy-start | bytes 1179652
  7.2 12.3 %copy-start.3 = (s32[16,256]{1,0:T(8,128)S(1)}, s32[16,256]{1,0:T(8,128)}, u32[]{:S(2)}) copy-start(s32[16,256]{1,0:T(8,128)} %param.11) | copy-start | bytes 49156
  7.2 12.4 %copy-start.2 = (f32[3,3,16,256]{3,2,1,0:T(8,128)S(1)}, f32[3,3,16,256]{3,2,1,0:T(8,128)}, u32[]{:S(2)}) copy-start(f32[3,3,16,256]{3,2,1,0:T(8,128)} %param.9) | copy-start | bytes 442372
  7.2 150.6 %all-reduce.4.cloned.1.call-start = ((), (), s32[]{:S(2)}) async-start(), calls=%async_computation | async-start | bytes 3145728 | tf_op jit(solution)/shard_map/psum | solution.py:88
  8.6 11.7 %copy-start.4 = (f32[3,16,256]{2,1,0:T(8,128)S(1)}, f32[3,16,256]{2,1,0:T(8,128)}, u32[]{:S(2)}) copy-start(f32[3,16,256]{2,1,0:T(8,128)} %param.10) | copy-start | bytes 147460
  8.8 13.3 %collective-permute-start.1 = (bf16[3,128,256]{2,0,1:T(4,128)(2,1)S(1)}, bf16[3,128,256]{2,0,1:T(4,128)(2,1)}, u32[]{:S(2)}, u32[]{:S(2)}) collective-permute-start(bf16[3,128,256]{2,0,1:T(4,128)(2,1)S(1)} %get-tuple-element.39), channel_id=1, source_target_pairs={{8,0},{16,8},{24,16},{32,24},{40,32},{48,40},{56,48},{64,56},{72,6... | collective-permute-start | bytes 589832 | tf_op jit(solution)/shard_map/ppermute | solution.py:22
  13.8 10.3 %collective-permute-start = (bf16[3,128,256]{2,0,1:T(4,128)(2,1)S(1)}, bf16[3,128,256]{2,0,1:T(4,128)(2,1)}, u32[]{:S(2)}, u32[]{:S(2)}) collective-permute-start(bf16[3,128,256]{2,0,1:T(4,128)(2,1)S(1)} %get-tuple-element.38), channel_id=1, source_target_pairs={{0,8},{8,16},{16,24},{24,32},{32,40},{40,48},{48,56},{56,64},{64,7... | collective-permute-start | bytes 589832 | tf_op jit(solution)/shard_map/ppermute | solution.py:21
  14.7 53.3 %collective-permute-start.3 = (bf16[3,256,128]{2,1,0:T(8,128)(2,1)}, bf16[3,256,128]{2,1,0:T(8,128)(2,1)}, u32[]{:S(2)}, u32[]{:S(2)}) collective-permute-start(bf16[3,256,128]{2,1,0:T(8,128)(2,1)} %get-tuple-element.41), channel_id=1, source_target_pairs={{1,0},{2,1},{3,2},{4,3},{5,4},{6,5},{7,6},{9,8},{10,9},{11,10},{12... | collective-permute-start | bytes 589832 | tf_op jit(solution)/shard_map/ppermute | solution.py:22
  18.2 49.7 %collective-permute-start.2 = (bf16[3,256,128]{2,1,0:T(8,128)(2,1)}, bf16[3,256,128]{2,1,0:T(8,128)(2,1)}, u32[]{:S(2)}, u32[]{:S(2)}) collective-permute-start(bf16[3,256,128]{2,1,0:T(8,128)(2,1)} %get-tuple-element.40), channel_id=1, source_target_pairs={{0,1},{1,2},{2,3},{3,4},{4,5},{5,6},{6,7},{8,9},{9,10},{10,11},{11... | collective-permute-start | bytes 589832 | tf_op jit(solution)/shard_map/ppermute | solution.py:21
  25.9 32.8 %copy-start.1 = (f32[3,16,256]{1,0,2:T(4,128)S(1)}, f32[3,16,256]{1,0,2:T(4,128)}, u32[]{:S(2)}) copy-start(f32[3,16,256]{1,0,2:T(4,128)} %copy.16) | copy-start | bytes 147460
  71.0 0.7 copy-start.5
  71.0 11.3 %copy-start.7 = (u32[128]{0:T(128)S(1)}, u32[128]{0:T(128)}, u32[]{:S(2)}) copy-start(u32[128]{0:T(128)} %constant.93) | copy-start | bytes 1540
  71.0 12.0 %copy-start.6 = (s32[2,256]{1,0:T(2,128)S(1)}, s32[2,256]{1,0:T(2,128)}, u32[]{:S(2)}) copy-start(s32[2,256]{1,0:T(2,128)} %param.12) | copy-start | bytes 6148
Sparse Core Ops, SparseCore 0:
  71.1 86.6 all-reduce.3
where the time goes:
time: 191 us
  waiting for transfers between devices  76.9 us (40%)
  local copies, waits for them, and re-layouts  44.7 us (23%)
  blocking collectives  20.6 us (11%)
  between operations  15.5 us (8%)
  matrix products  12.2 us (6%)
  starting transfers between devices  9.86 us (5%)
  other arithmetic  6.15 us (3%)
  loops' own time  5 us (3%)
    psum x1, waiting for transfers between devices, body(): summed_pair = lax.psum(pair_terms, 'atom')  74.9 us
    gather x1, local copies, waits for them, and re-layouts, body(): gathered = jnp.take(row_major, local_ids, axis=0)  32.8 us
    unnamed x1, blocking collectives  11.9 us
    dot_general x1, matrix products, body(): jnp.einsum('kcdna,nadi->kcai', coupling, gathered, preferred_element_type...  9.23 us
    all_gather x1, blocking collectives, body(): spectrum = lax.all_gather(freq, 'mode', axis=0, tiled=True)  8.7 us
    ppermute x2, starting transfers between devices, extended(): after = lax.ppermute(first, axis, down)  8.54 us
    unnamed x23, local copies, waits for them, and re-layouts  5.23 us
    another operation x1, loops' own time, prefix(): return lax.fori_loop(0, place, one, state)  5 us
  transfers between devices with their start and end apart: 5, of which 2 were waited for; matrix products, arithmetic and copies ran while one was open for 25% of the time, Pallas kernels for 0%

commit v1 on v0

--- a/solution.py
+++ b/solution.py
@@ -3,6 +3,7 @@
 import jax.numpy as jnp
 from jax import lax
 from jax.sharding import PartitionSpec as P
+from jax.lax import all_gather
 
 ATOM_DEV = 256
 MODE_DEV = 256
@@ -85,7 +86,7 @@
     partner_ids = mode_start - HALF + jnp.arange(partner_span, dtype=jnp.int32)
     own_ids = mode_start + jnp.arange(MODE_DEV, dtype=jnp.int32)
     weight = pair_weight(freq, partner_freq, own_ids, partner_ids, band[0], band[1], broaden)
-    summed_pair = lax.psum(pair_terms, "atom")
+    summed_pair = jnp.sum(all_gather(pair_terms, axis_name="atom"), axis=0)
     strength = jnp.sum(summed_pair * summed_pair, axis=0)
     row_sums = jnp.sum(weight * strength, axis=0)
     diffusivity = math.pi / (3.0 * freq * freq) * row_sums

time: 191 us -> 267 us (1.40)
  waiting for transfers between devices: 76.9 us -> 144 us
  other arithmetic: 6.15 us -> 14 us
    all_gather x0 -> x1, waiting for transfers between devices: none -> 141 us  [body(): summed_pair = jnp.sum(all_gather(pair_terms, axis_name='atom'), axis=0)]
    psum x1 -> x0, waiting for transfers between devices: 74.9 us -> none  [body(): summed_pair = lax.psum(pair_terms, 'atom')]
    reduce_sum x0 -> x1, other arithmetic: none -> 9.32 us  [body(): summed_pair = jnp.sum(all_gather(pair_terms, axis_name='atom'), axis=0)]
    unnamed x23 -> x24, local copies, waits for them, and re-layouts: 5.23 us -> 5.58 us
  transfers between devices with their start and end apart: 5 -> 5, of which waited for: 2 -> 2; matrix products, arithmetic and copies ran while one was open for 25% -> 18% of each run, Pallas kernels for 0% -> 0%
where the time goes in v1:
time: 267 us; the launch traced here: 266 us
  waiting for transfers between devices  144 us (54%)
  local copies, waits for them, and re-layouts  46.8 us (18%)
  blocking collectives  20.6 us (8%)
  between operations  15.6 us (6%)
  other arithmetic  14 us (5%)
  matrix products  11.1 us (4%)
  starting transfers between devices  9.86 us (4%)
  loops' own time  5 us (2%)
    all_gather x1, waiting for transfers between devices, body(): summed_pair = jnp.sum(all_gather(pair_terms, axis_name='atom'), axis=0)  141 us
    gather x1, local copies, waits for them, and re-layouts, body(): gathered = jnp.take(row_major, local_ids, axis=0)  32.8 us
    unnamed x1, blocking collectives  11.9 us
    reduce_sum x1, other arithmetic, body(): summed_pair = jnp.sum(all_gather(pair_terms, axis_name='atom'), axis=0)  9.32 us
    dot_general x1, matrix products, body(): jnp.einsum('kcdna,nadi->kcai', coupling, gathered, preferred_element_type...  9.23 us
    all_gather x1, blocking collectives, body(): spectrum = lax.all_gather(freq, 'mode', axis=0, tiled=True)  8.7 us
    ppermute x2, starting transfers between devices, extended(): after = lax.ppermute(first, axis, down)  8.54 us
    unnamed x24, local copies, waits for them, and re-layouts  5.58 us
  transfers between devices with their start and end apart: 5, of which 2 were waited for; matrix products, arithmetic and copies ran while one was open for 18% of the time, Pallas kernels for 0%

profile of v1, /device:TPU:97, one launch (start us, length us, event | category | flops | bytes accessed | tf_op | source)
XLA Modules:
  0.0 266.3 jit_solution(3875908340183067456)
XLA Ops:
  7.2 1.4 copy.22
  8.8 5.0 %collective-permute-start.1 = (bf16[3,128,256]{2,0,1:T(4,128)(2,1)S(1)}, bf16[3,128,256]{2,0,1:T(4,128)(2,1)}, u32[]{:S(2)}, u32[]{:S(2)}) collective-permute-start(bf16[3,128,256]{2,0,1:T(4,128)(2,1)S(1)} %get-tuple-element.39), channel_id=1, source_target_pairs={{8,0},{16,8},{24,16},{32,24},{40,32},{48,40},{56,48},{64,56},{72,6... | collective-permute-start | bytes 589832 | tf_op jit(solution)/shard_map/ppermute | solution.py:23
  13.8 0.9 fusion.22
  14.7 3.5 %collective-permute-start.3 = (bf16[3,256,128]{2,1,0:T(8,128)(2,1)}, bf16[3,256,128]{2,1,0:T(8,128)(2,1)}, u32[]{:S(2)}, u32[]{:S(2)}) collective-permute-start(bf16[3,256,128]{2,1,0:T(8,128)(2,1)} %get-tuple-element.41), channel_id=1, source_target_pairs={{1,0},{2,1},{3,2},{4,3},{5,4},{6,5},{7,6},{9,8},{10,9},{11,10},{12... | collective-permute-start | bytes 589832 | tf_op jit(solution)/shard_map/ppermute | solution.py:23
  18.2 1.3 collective-permute-start.2
  19.6 0.7 copy.27
  20.4 1.1 copy.26
  21.4 0.7 copy.21
  22.1 2.0 collective-permute-done
  24.2 1.8 maximum_bitcast_fusion
  25.9 32.8 %gather_fusion = bf16[4096,3,256]{2,1,0:T(4,128)(2,1)} fusion(bf16[512,3,256]{2,1,0:T(4,128)(2,1)S(1)} %maximum_bitcast_fusion, s32[4096]{0:T(1024)S(1)} %broadcast_clamp_fusion), kind=kCustom, calls=%fused_computation | custom fusion | bytes 12599296 | tf_op jit(solution)/shard_map/jit(_take)/gather | solution.py:72
  58.7 9.2 %fusion.8 = bf16[3,3,256,256]{3,1,0,2:T(4,128)(2,1)S(1)} fusion(f32[3,3,16,256]{2,0,1,3:T(4,128)S(1)} %copy.27, f32[3,16,256]{1,0,2:T(4,128)S(1)} %copy-done.1, bf16[16,256,3,256]{3,2,1,0:T(4,128)(2,1)} %bitcast.44, pred[16,256]{0,1:T(8,128)(4,1)} %copy.21), kind=kOutput, calls=%fused_computation.11 | convolution fusion | flops 60579840 | bytes 7671808 | tf_op jit(solution)/shard_map/kcdna,nadi->kcai/dot_general | solution.py:76
  68.0 1.8 convolution_bitcast_fusion
  69.8 1.7 copy.29
  71.5 0.6 copy-done.5
  72.2 8.7 %all-gather.1 = f32[8,1,256]{2,1,0:T(1,128)S(1)} all-gather(f32[1,1,256]{2,1,0:T(1,128)S(1)} %bitcast.47), channel_id=1, replica_groups=mesh['atom'=16,'mode'=8] {'mode'}, dimensions={0}, use_global_device_ids=true | all-gather | bytes 9216 | tf_op jit(solution)/shard_map/all_gather | solution.py:65
  80.9 0.6 fusion.20
  82.8 0.6 dynamic-slice
  83.5 141.5 %all-gather.4.cloned.1.call-done = f32[48,512,256]{2,1,0:T(8,128)} async-done(((f32[3,512,256]{2,1,0:T(8,128)}), f32[48,512,256]{2,1,0:T(8,128)}) %all-gather.4.cloned.1.call-update) | async-done | bytes 25165840 | tf_op jit(solution)/shard_map/all_gather | solution.py:89
  225.0 9.3 %reduce_sum.27 = f32[3,512,256]{2,1,0:T(8,128)S(1)} reduce(f32[16,3,512,256]{3,2,1,0:T(8,128)} %bitcast.43, f32[]{:T(128)} %copy.54), dimensions={0}, to_apply=%region_2.3 | reduce | flops 5898240 | bytes 26738692 | tf_op jit(solution)/shard_map/reduce_sum | solution.py:89
  235.5 0.6 multiply_bitcast_fusion
  236.7 0.7 slice_dynamic-update-slice_fusion
  237.4 11.9 %all-reduce.1 = f32[8]{0:T(128)S(1)} all-reduce(f32[8]{0:T(128)S(1)} %slice_dynamic-update-slice_fusion), channel_id=1, replica_groups=mesh['atom'=16,'mode'=8] {'mode'}, use_global_device_ids=true, to_apply=%add.1 | all-reduce | flops 8 | bytes 64
  249.3 9.7 %while.10 = (s32[]{:T(128)}, f32[]{:T(128)}, s32[]{:T(128)}, f32[8]{0:T(128)S(1)}, s32[]{:T(128)}, /*index=5*/s32[]{:T(128)}, s32[]{:T(128)}) while((s32[]{:T(128)}, f32[]{:T(128)}, s32[]{:T(128)}, f32[8]{0:T(128)S(1)}, s32[]{:T(128)}, /*index=5*/s32[]{:T(128)}, s32[]{:T(128)}) %tuple.27), condition=%wide.region_8.9_spmd, body=%wide.region_7.8_spmd.sunk | while | flops 6 | bytes 143 | solution.py:36
  249.3 0.7 dynamic_slice.10
  250.6 0.7 dynamic_slice.10
  252.0 0.7 dynamic_slice.10
  253.4 0.7 dynamic_slice.10
  254.8 0.7 dynamic_slice.10
  256.2 0.7 dynamic_slice.10
  257.6 0.7 dynamic_slice.10
  258.9 0.6 add_multiply_fusion
  (40 shorter events, 2.2 us)
Async XLA Ops:
  7.2 6.7 %copy-start = (bf16[3,256,256]{2,1,0:T(8,128)(2,1)S(1)}, bf16[3,256,256]{2,1,0:T(8,128)(2,1)}, u32[]{:S(2)}) copy-start(bf16[3,256,256]{2,1,0:T(8,128)(2,1)} %param.8) | copy-start | bytes 1179652
  7.2 12.4 %copy-start.3 = (s32[16,256]{1,0:T(8,128)S(1)}, s32[16,256]{1,0:T(8,128)}, u32[]{:S(2)}) copy-start(s32[16,256]{1,0:T(8,128)} %param.11) | copy-start | bytes 49156
  7.2 12.4 %copy-start.2 = (f32[3,3,16,256]{3,2,1,0:T(8,128)S(1)}, f32[3,3,16,256]{3,2,1,0:T(8,128)}, u32[]{:S(2)}) copy-start(f32[3,3,16,256]{3,2,1,0:T(8,128)} %param.9) | copy-start | bytes 442372
  7.2 217.8 %all-gather.4.cloned.1.call-start = ((), (), s32[]{:S(2)}) async-start(), calls=%async_computation | async-start | bytes 26738688 | tf_op jit(solution)/shard_map/all_gather | solution.py:89
  8.6 11.7 %copy-start.4 = (f32[3,16,256]{2,1,0:T(8,128)S(1)}, f32[3,16,256]{2,1,0:T(8,128)}, u32[]{:S(2)}) copy-start(f32[3,16,256]{2,1,0:T(8,128)} %param.10) | copy-start | bytes 147460
  8.8 13.3 %collective-permute-start.1 = (bf16[3,128,256]{2,0,1:T(4,128)(2,1)S(1)}, bf16[3,128,256]{2,0,1:T(4,128)(2,1)}, u32[]{:S(2)}, u32[]{:S(2)}) collective-permute-start(bf16[3,128,256]{2,0,1:T(4,128)(2,1)S(1)} %get-tuple-element.39), channel_id=1, source_target_pairs={{8,0},{16,8},{24,16},{32,24},{40,32},{48,40},{56,48},{64,56},{72,6... | collective-permute-start | bytes 589832 | tf_op jit(solution)/shard_map/ppermute | solution.py:23
  13.8 10.3 %collective-permute-start = (bf16[3,128,256]{2,0,1:T(4,128)(2,1)S(1)}, bf16[3,128,256]{2,0,1:T(4,128)(2,1)}, u32[]{:S(2)}, u32[]{:S(2)}) collective-permute-start(bf16[3,128,256]{2,0,1:T(4,128)(2,1)S(1)} %get-tuple-element.38), channel_id=1, source_target_pairs={{0,8},{8,16},{16,24},{24,32},{32,40},{40,48},{48,56},{56,64},{64,7... | collective-permute-start | bytes 589832 | tf_op jit(solution)/shard_map/ppermute | solution.py:22
  14.7 53.2 %collective-permute-start.3 = (bf16[3,256,128]{2,1,0:T(8,128)(2,1)}, bf16[3,256,128]{2,1,0:T(8,128)(2,1)}, u32[]{:S(2)}, u32[]{:S(2)}) collective-permute-start(bf16[3,256,128]{2,1,0:T(8,128)(2,1)} %get-tuple-element.41), channel_id=1, source_target_pairs={{1,0},{2,1},{3,2},{4,3},{5,4},{6,5},{7,6},{9,8},{10,9},{11,10},{12... | collective-permute-start | bytes 589832 | tf_op jit(solution)/shard_map/ppermute | solution.py:23
  18.2 49.7 %collective-permute-start.2 = (bf16[3,256,128]{2,1,0:T(8,128)(2,1)}, bf16[3,256,128]{2,1,0:T(8,128)(2,1)}, u32[]{:S(2)}, u32[]{:S(2)}) collective-permute-start(bf16[3,256,128]{2,1,0:T(8,128)(2,1)} %get-tuple-element.40), channel_id=1, source_target_pairs={{0,1},{1,2},{2,3},{3,4},{4,5},{5,6},{6,7},{8,9},{9,10},{10,11},{11... | collective-permute-start | bytes 589832 | tf_op jit(solution)/shard_map/ppermute | solution.py:22
  25.9 32.8 %copy-start.1 = (f32[3,16,256]{1,0,2:T(4,128)S(1)}, f32[3,16,256]{1,0,2:T(4,128)}, u32[]{:S(2)}) copy-start(f32[3,16,256]{1,0,2:T(4,128)} %copy.26) | copy-start | bytes 147460
  71.5 0.7 copy-start.5
  71.5 11.3 %copy-start.7 = (u32[128]{0:T(128)S(1)}, u32[128]{0:T(128)}, u32[]{:S(2)}) copy-start(u32[128]{0:T(128)} %constant.93) | copy-start | bytes 1540
  71.5 12.0 %copy-start.6 = (s32[2,256]{1,0:T(2,128)S(1)}, s32[2,256]{1,0:T(2,128)}, u32[]{:S(2)}) copy-start(s32[2,256]{1,0:T(2,128)} %param.12) | copy-start | bytes 6148
Sparse Core Ops, SparseCore 0:
  71.7 153.2 all-gather.3
